TPU v7x, 512 devices: a whole 4x4x16 slice. The times are simulated.
512 devices in a mesh: ktot: 32 (over z_lo, y, core), kvir: 16 (over z_hi, x).
Axes of the slice: x: 4, y: 4, z: 16 (z_hi: 4, z_lo: 4; z = z_hi * 4 + z_lo), core: 2. Of those that a mesh axis runs over, the one named last changes fastest.
Arguments:
- amplitudes: bfloat16 [32, 16, 672, 1024], P('ktot', 'kvir'), may hold values from -6 to 6
- ladder_integrals: bfloat16 [32, 16, 1024, 1024], P('ktot', 'kvir'), may hold values from -0.046875 to 0.046875
- listed: int32 [32, 16], P('ktot', 'kvir'), may hold values 0 or 1
- current: bfloat16 [32, 672, 1024], P('ktot', 'kvir'), may hold values from -3 to 3
- denominators: float32 [32, 672, 1024], P('ktot', 'kvir'), may hold values from 2 to 8
- cycle_integrals: bfloat16 [32, 512, 512], P('ktot', 'kvir'), may hold values from -0.25 to 0.25
Outputs:
- ladder_res: bfloat16 [32, 672, 1024], P('ktot', 'kvir')
- cycle_res: float32 [32, 1344, 1344], P('ktot', 'kvir')
All inputs are finite; a program needn't handle non-finite values. No bound on the sum of `listed` on one device may be relied on, other than what follows from the above.
Results may differ from a plain program's by a relative error of at most 0.017.
Values may be sent and summed in bfloat16 or wider, within the bound.
No kernel may reach another device: no remote copies, remote signals or barrier semaphores. Data moves between devices by JAX's collectives and lax.ppermute only.
A program may use at most 64 MiB of HBM per device.

v0:
```python
import jax
import jax.numpy as jnp
from jax import lax
from jax.sharding import PartitionSpec as P


def shards(amplitudes, ladder_integrals, listed, current, denominators, cycle_integrals):
    amp_block = amplitudes[0, 0]
    weights = ladder_integrals[0, 0]
    scale_mask = listed[0, 0].astype(jnp.float32)
    rows_dev = current.shape[1]
    width = current.shape[2]
    tot_count = lax.axis_size("ktot")
    vir_count = lax.axis_size("kvir")
    summed = lax.psum(
        jnp.dot(amp_block, weights, preferred_element_type=jnp.float32) * scale_mask, "kvir"
    )
    ladder = lax.dynamic_slice_in_dim(summed, lax.axis_index("kvir") * rows_dev, rows_dev, 0)
    updated = (current[0].astype(jnp.float32) + ladder / denominators[0]).astype(jnp.bfloat16)
    col_width = width // tot_count
    received = lax.all_to_all(
        updated.reshape(rows_dev, tot_count, col_width),
        "ktot",
        split_axis=1,
        concat_axis=1,
        tiled=True,
    )
    local_cycle = received.reshape(rows_dev * tot_count, col_width)
    cycle_rows = local_cycle.shape[0]
    cycle_weights = cycle_integrals[0]
    cycle_width = cycle_weights.shape[1]
    share_rows = cycle_rows // vir_count
    my_start = lax.axis_index("kvir") * share_rows
    partial_cycle = jnp.dot(local_cycle, cycle_weights, preferred_element_type=jnp.float32)
    partial_cycle = partial_cycle.astype(jnp.bfloat16).astype(jnp.float32)
    summed_cycle = lax.psum(partial_cycle.astype(jnp.bfloat16), "kvir").astype(jnp.float32)
    cycle_mixed = lax.dynamic_slice_in_dim(summed_cycle, my_start, share_rows, 0).astype(
        jnp.bfloat16
    )
    cycle_out = lax.dot_general(
        cycle_mixed,
        lax.all_gather(local_cycle, "kvir", axis=1, tiled=True),
        (((1,), (1,)), ((), ())),
        preferred_element_type=jnp.float32,
    )
    return (ladder.astype(jnp.bfloat16)[None], (cycle_out * cycle_width ** (-0.5))[None])


def solution(mesh):
    return jax.shard_map(
        shards,
        mesh=mesh,
        in_specs=(
            P("ktot", "kvir", None, None),
            P("ktot", "kvir", None, None),
            P("ktot", "kvir"),
            P("ktot", "kvir", None),
            P("ktot", "kvir", None),
            P("ktot", "kvir", None),
        ),
        out_specs=(P("ktot", "kvir", None), P("ktot", "kvir", None)),
        check_vma=False,
    )
```

profile of v0, /device:TPU:8, one launch (start us, length us, event | category | flops | bytes accessed | tf_op | source)
XLA Modules:
  0.0 652.3 jit_solution(10469983389552584151)
XLA Ops:
  7.2 0.0 copy-start
  7.2 0.0 all-reduce.3.cloned.1.call-start
  8.0 0.8 copy-done
  8.8 4.5 fusion.3
  13.3 0.0 copy-start.2
  13.3 0.0 copy-start.3
  13.3 0.0 all-reduce.3.cloned.1.call-update
  13.3 0.0 all-reduce.5.cloned.1.call-start
  13.4 0.0 copy-start.4
  13.4 298.0 %all-reduce.3.cloned.1.call-done = f32[672,1024]{1,0:T(8,128)} async-done(((f32[672,1024]{1,0:T(8,128)}), f32[672,1024]{1,0:T(8,128)}) %all-reduce.3.cloned.1.call-update) | async-done | bytes 2752528 | tf_op jit(solution)/shard_map/psum | solution.py:15
  311.4 0.0 copy-done.2
  311.4 0.0 copy-done.3
  311.4 1.0 fusion.8
  312.4 0.2 copy.15
  312.6 0.4 reshape.16
  312.9 18.6 %all_to_all.5 = bf16[32,2,672]{2,1,0:T(2,128)(2,1)S(1)} all-to-all(bf16[32,2,672]{2,1,0:T(2,128)(2,1)S(1)} %reshape.16), channel_id=1, replica_groups=mesh['ktot'=32,'kvir'=16] {'ktot'}, dimensions={0} | all-to-all | bytes 172032 | tf_op jit(solution)/shard_map/all_to_all | solution.py:21
  331.6 0.4 reshape.17
  332.0 0.4 copy.13
  332.4 0.3 reshape.14
  332.7 0.0 copy-start.1
  332.7 0.0 copy-done.4
  332.7 1.6 convolution_convert_fusion
  334.4 0.0 all-reduce.5.cloned.1.call-update
  334.4 0.0 all-gather.2.cloned.1.call-start
  334.4 0.0 copy-done.1
  334.5 0.7 all-gather.2.cloned.1.call-update
  335.1 1.6 fusion.9
  336.7 219.6 %all-reduce.5.cloned.1.call-done = bf16[1344,512]{1,0:T(8,128)(2,1)} async-done(((bf16[1344,512]{1,0:T(8,128)(2,1)}), bf16[1344,512]{1,0:T(8,128)(2,1)}) %all-reduce.5.cloned.1.call-update) | async-done | bytes 1376272 | tf_op jit(solution)/shard_map/psum | solution.py:36
  556.3 86.4 %all-gather.2.cloned.1.call-done = bf16[1344,512]{0,1:T(8,128)(2,1)} async-done(((bf16[1344,32]{0,1:T(8,128)(2,1)}), bf16[1344,512]{0,1:T(8,128)(2,1)}) %all-gather.2.cloned.1.call-update) | async-done | bytes 1376272 | tf_op jit(solution)/shard_map/all_gather | solution.py:42
  642.7 1.8 fusion
  644.5 1.3 copy.14
Async XLA Ops:
  7.2 1.6 copy-start
  7.2 304.2 %all-reduce.3.cloned.1.call-start = ((), (), s32[]{:S(2)}) async-start(), calls=%async_computation.1 | async-start | bytes 5505024 | tf_op jit(solution)/shard_map/psum | solution.py:15
  13.3 298.1 %copy-start.2 = (f32[1,42,1024]{2,0,1:T(1,128)S(1)}, f32[1,42,1024]{2,0,1:T(1,128)}, u32[]{:S(2)}) copy-start(f32[1,42,1024]{2,0,1:T(1,128)} %param.10) | copy-start | bytes 516100
  13.3 298.1 %copy-start.3 = (bf16[1,42,1024]{2,1,0:T(8,128)(2,1)S(1)}, bf16[1,42,1024]{2,1,0:T(8,128)(2,1)}, u32[]{:S(2)}) copy-start(bf16[1,42,1024]{2,1,0:T(8,128)(2,1)} %param.9) | copy-start | bytes 258052
  13.3 542.9 %all-reduce.5.cloned.1.call-start = ((), (), s32[]{:S(2)}) async-start(), calls=%async_computation.2 | async-start | bytes 2752512 | tf_op jit(solution)/shard_map/psum | solution.py:36
  13.4 319.3 %copy-start.4 = (bf16[1,32,512]{2,1,0:T(8,128)(2,1)S(1)}, bf16[1,32,512]{2,1,0:T(8,128)(2,1)}, u32[]{:S(2)}) copy-start(bf16[1,32,512]{2,1,0:T(8,128)(2,1)} %param.11) | copy-start | bytes 98308
  332.7 1.7 copy-start.1
  334.4 308.3 %all-gather.2.cloned.1.call-start = ((), (), s32[]{:S(2)}) async-start(), calls=%async_computation.3 | async-start | bytes 1531904 | tf_op jit(solution)/shard_map/all_gather | solution.py:42
Sparse Core Ops, SparseCore 0:
  13.5 297.8 all-reduce.2
  334.5 221.7 all-reduce.4
  559.9 82.7 all-gather.1
where the time goes:
time: 653 us; the launch traced here: 652 us
  waiting for transfers between devices  605 us (93%)
  blocking collectives  18.6 us (3%)
  between operations  14.6 us (2%)
  matrix products  7.95 us (1%)
    psum x1, waiting for transfers between devices, shards(): lax.psum(jnp.dot(amp_block, weights, preferred_element_type=jnp.float32)...  298 us
    psum x1, waiting for transfers between devices, shards(): lax.psum(partial_cycle.astype(jnp.bfloat16), 'kvir').astype(jnp.float32)  220 us
    all_gather x1, waiting for transfers between devices, shards(): lax.all_gather(local_cycle, 'kvir', axis=1, tiled=True)  86.4 us
    all_to_all x1, blocking collectives, shards(): lax.all_to_all(updated.reshape(rows_dev, tot_count, col_width), 'ktot', s...  18.6 us
  transfers between devices with their start and end apart: 3, of which 3 were waited for; matrix products, arithmetic and copies ran while one was open for 0% of the time, Pallas kernels for 0%

commit v1 on v0

--- a/solution.py
+++ b/solution.py
@@ -12,8 +12,11 @@
     width = current.shape[2]
     tot_count = lax.axis_size("ktot")
     vir_count = lax.axis_size("kvir")
-    summed = lax.psum(
-        jnp.dot(amp_block, weights, preferred_element_type=jnp.float32) * scale_mask, "kvir"
+    summed = jnp.sum(
+        lax.all_gather(
+            jnp.dot(amp_block, weights, preferred_element_type=jnp.float32) * scale_mask, "kvir"
+        ),
+        axis=0,
     )
     ladder = lax.dynamic_slice_in_dim(summed, lax.axis_index("kvir") * rows_dev, rows_dev, 0)
     updated = (current[0].astype(jnp.float32) + ladder / denominators[0]).astype(jnp.bfloat16)

time: 653 us -> 1310 us (2.01)
  waiting for transfers between devices: 605 us -> 1150 us
  blocking collectives: 18.6 us -> 120 us
  other arithmetic: 1 us -> 18.4 us
    all_gather x0 -> x1, waiting for transfers between devices: none -> 839 us  [shards(): lax.all_gather(jnp.dot(amp_block, weights, preferred_element_type=jnp.flo...]
    psum x1 -> x0, waiting for transfers between devices: 298 us -> none  [shards(): lax.psum(jnp.dot(amp_block, weights, preferred_element_type=jnp.float32)...]
    all_to_all x1, blocking collectives: 18.6 us -> 120 us  [shards(): lax.all_to_all(updated.reshape(rows_dev, tot_count, col_width), 'ktot', s...]
    reduce_sum x0 -> x1, other arithmetic: none -> 17.4 us  [shards(): jnp.sum(lax.all_gather(jnp.dot(amp_block, weights, preferred_element_type...]
where the time goes in v1:
time: 1310 us
  waiting for transfers between devices  1150 us (88%)
  blocking collectives  120 us (9%)
  other arithmetic  18.4 us (1%)
  between operations  14.6 us (1%)
    all_gather x1, waiting for transfers between devices, shards(): lax.all_gather(jnp.dot(amp_block, weights, preferred_element_type=jnp.flo...  839 us
    psum x1, waiting for transfers between devices, shards(): lax.psum(partial_cycle.astype(jnp.bfloat16), 'kvir').astype(jnp.float32)  219 us
    all_to_all x1, blocking collectives, shards(): lax.all_to_all(updated.reshape(rows_dev, tot_count, col_width), 'ktot', s...  120 us
    all_gather x1, waiting for transfers between devices, shards(): lax.all_gather(local_cycle, 'kvir', axis=1, tiled=True)  86.4 us
  transfers between devices with their start and end apart: 3, of which 3 were waited for; matrix products, arithmetic and copies ran while one was open for 0% of the time, Pallas kernels for 0%

profile of v1, /device:TPU:8, one launch (start us, length us, event | category | flops | bytes accessed | tf_op | source)
XLA Modules:
  0.0 1311.6 jit_solution(13449652044428111938)
XLA Ops:
  7.2 0.0 copy-start
  7.2 0.0 all-gather.6.cloned.1.call-start
  8.0 0.8 copy-done
  8.8 4.5 fusion.3
  13.3 0.0 all-gather.6.cloned.1.call-update
  13.3 0.0 all-reduce.2.cloned.1.call-start
  13.3 838.9 %all-gather.6.cloned.1.call-done = f32[10752,1024]{1,0:T(8,128)} async-done(((f32[672,1024]{1,0:T(8,128)}), f32[10752,1024]{1,0:T(8,128)}) %all-gather.6.cloned.1.call-update) | async-done | bytes 44040208 | tf_op jit(solution)/shard_map/all_gather | solution.py:16
  852.3 0.0 copy-start.2
  852.3 0.0 copy-start.3
  852.3 17.4 %reduce_sum.9 = f32[672,1024]{1,0:T(8,128)} reduce(f32[16,672,1024]{2,1,0:T(8,128)} %bitcast.33, f32[]{:T(128)} %constant.8.clone.1), dimensions={0}, to_apply=%region_0.0 | reduce | flops 10321920 | bytes 46792708 | tf_op jit(solution)/shard_map/reduce_sum | solution.py:15
  869.7 0.0 copy-done.2
  869.7 0.0 copy-done.3
  869.7 0.0 copy-start.4
  869.7 1.0 fusion.8
  870.7 0.2 copy.15
  870.9 0.4 reshape.17
  871.2 120.1 %all_to_all.5 = bf16[32,2,672]{2,1,0:T(2,128)(2,1)S(1)} all-to-all(bf16[32,2,672]{2,1,0:T(2,128)(2,1)S(1)} %reshape.17), channel_id=1, replica_groups=mesh['ktot'=32,'kvir'=16] {'ktot'}, dimensions={0} | all-to-all | bytes 172032 | tf_op jit(solution)/shard_map/all_to_all | solution.py:24
  991.3 0.4 reshape.18
  991.7 0.4 copy.13
  992.2 0.3 reshape.14
  992.4 0.0 copy-start.1
  992.5 0.0 copy-done.4
  992.5 1.6 convolution_convert_fusion
  994.1 0.0 all-reduce.2.cloned.1.call-update
  994.1 0.0 all-gather.4.cloned.1.call-start
  994.2 0.0 copy-done.1
  994.2 0.7 all-gather.4.cloned.1.call-update
  994.8 1.6 fusion.9
  996.5 219.2 %all-reduce.2.cloned.1.call-done = bf16[1344,512]{1,0:T(8,128)(2,1)} async-done(((bf16[1344,512]{1,0:T(8,128)(2,1)}), bf16[1344,512]{1,0:T(8,128)(2,1)}) %all-reduce.2.cloned.1.call-update) | async-done | bytes 1376272 | tf_op jit(solution)/shard_map/psum | solution.py:39
  1215.6 86.4 %all-gather.4.cloned.1.call-done = bf16[1344,512]{0,1:T(8,128)(2,1)} async-done(((bf16[1344,32]{0,1:T(8,128)(2,1)}), bf16[1344,512]{0,1:T(8,128)(2,1)}) %all-gather.4.cloned.1.call-update) | async-done | bytes 1376272 | tf_op jit(solution)/shard_map/all_gather | solution.py:45
  1302.0 1.8 fusion
  1303.8 1.3 copy.14
Async XLA Ops:
  7.2 1.6 copy-start
  7.2 845.1 %all-gather.6.cloned.1.call-start = ((), (), s32[]{:S(2)}) async-start(), calls=%async_computation.3 | async-start | bytes 46792704 | tf_op jit(solution)/shard_map/all_gather | solution.py:16
  13.3 1202.4 %all-reduce.2.cloned.1.call-start = ((), (), s32[]{:S(2)}) async-start(), calls=%async_computation.1 | async-start | bytes 2752512 | tf_op jit(solution)/shard_map/psum | solution.py:39
  852.3 17.4 %copy-start.2 = (f32[1,42,1024]{2,0,1:T(1,128)S(1)}, f32[1,42,1024]{2,0,1:T(1,128)}, u32[]{:S(2)}) copy-start(f32[1,42,1024]{2,0,1:T(1,128)} %param.10) | copy-start | bytes 516100
  852.3 17.4 %copy-start.3 = (bf16[1,42,1024]{2,1,0:T(8,128)(2,1)S(1)}, bf16[1,42,1024]{2,1,0:T(8,128)(2,1)}, u32[]{:S(2)}) copy-start(bf16[1,42,1024]{2,1,0:T(8,128)(2,1)} %param.9) | copy-start | bytes 258052
  869.7 122.8 %copy-start.4 = (bf16[1,32,512]{2,1,0:T(8,128)(2,1)S(1)}, bf16[1,32,512]{2,1,0:T(8,128)(2,1)}, u32[]{:S(2)}) copy-start(bf16[1,32,512]{2,1,0:T(8,128)(2,1)} %param.11) | copy-start | bytes 98308
  992.4 1.7 copy-start.1
  994.1 307.9 %all-gather.4.cloned.1.call-start = ((), (), s32[]{:S(2)}) async-start(), calls=%async_computation.2 | async-start | bytes 1531904 | tf_op jit(solution)/shard_map/all_gather | solution.py:45
Sparse Core Ops, SparseCore 0:
  13.4 838.8 all-gather.5
  994.2 221.3 all-reduce.1
  1219.2 82.7 all-gather.3

commit v2 on v0

--- a/solution.py
+++ b/solution.py
@@ -39,7 +39,9 @@
     )
     cycle_out = lax.dot_general(
         cycle_mixed,
-        lax.all_gather(local_cycle, "kvir", axis=1, tiled=True),
+        jnp.concatenate(
+            lax.all_to_all(jnp.stack([local_cycle] * lax.axis_size("kvir")), "kvir", 0, 0), axis=1
+        ),
         (((1,), (1,)), ((), ())),
         preferred_element_type=jnp.float32,
     )

time: 653 us -> 624 us (0.956)
  the two profiles are of different devices: /device:TPU:8 before, /device:TPU:16 now
where the time goes in v2:
time: 624 us
  waiting for transfers between devices  563 us (90%)
  blocking collectives  17.7 us (3%)
  between operations  14.9 us (2%)
  starting transfers between devices  12.1 us (2%)
  matrix products  8.3 us (1%)
  local copies, waits for them, and re-layouts  6.52 us (1%)
    psum x1, waiting for transfers between devices, shards(): lax.psum(jnp.dot(amp_block, weights, preferred_element_type=jnp.float32)...  298 us
    psum x1, waiting for transfers between devices, shards(): lax.psum(partial_cycle.astype(jnp.bfloat16), 'kvir').astype(jnp.float32)  265 us
    all_to_all x1, blocking collectives, shards(): lax.all_to_all(updated.reshape(rows_dev, tot_count, col_width), 'ktot', s...  17.7 us
  transfers between devices with their start and end apart: 3, of which 2 were waited for; matrix products, arithmetic and copies ran while one was open for 1% of the time, Pallas kernels for 0%

profile of v2, /device:TPU:16, one launch (start us, length us, event | category | flops | bytes accessed | tf_op | source)
XLA Modules:
  0.0 623.9 jit_solution(5741072749254752000)
XLA Ops:
  7.2 0.0 copy-start
  7.2 0.0 all-reduce.3.cloned.1.call-start
  8.0 0.8 copy-done
  8.8 4.5 fusion.3
  13.3 0.0 copy-start.2
  13.3 0.0 copy-start.3
  13.3 0.0 all-reduce.3.cloned.1.call-update
  13.3 297.8 %all-reduce.3.cloned.1.call-done = f32[672,1024]{1,0:T(8,128)} async-done(((f32[672,1024]{1,0:T(8,128)}), f32[672,1024]{1,0:T(8,128)}) %all-reduce.3.cloned.1.call-update) | async-done | bytes 2752528 | tf_op jit(solution)/shard_map/psum | solution.py:15
  311.2 0.0 copy-done.2
  311.2 0.0 copy-done.3
  311.2 1.0 fusion.8
  312.2 0.2 copy.16
  312.4 0.4 reshape.26
  312.7 17.7 %all_to_all.10 = bf16[32,2,672]{2,1,0:T(2,128)(2,1)S(1)} all-to-all(bf16[32,2,672]{2,1,0:T(2,128)(2,1)S(1)} %reshape.26), channel_id=1, replica_groups=mesh['ktot'=32,'kvir'=16] {'ktot'}, dimensions={0} | all-to-all | bytes 172032 | tf_op jit(solution)/shard_map/all_to_all | solution.py:21
  330.4 0.4 reshape.27
  330.8 0.4 copy.14
  331.2 0.3 reshape.22
  331.5 0.0 copy-start.1
  331.5 1.2 stack.3
  332.7 0.0 copy-done.1
  332.8 12.1 %all-to-all-start.1 = ((bf16[16,1344,32]{1,2,0:T(8,128)(2,1)}), bf16[16,1344,32]{1,2,0:T(8,128)(2,1)S(1)}, u32[]{:S(2)}, u32[]{:S(2)}) async-start(bf16[16,1344,32]{1,2,0:T(8,128)(2,1)} %stack.3), calls=%async_computation.1 | async-start | bytes 2883584 | tf_op jit(solution)/shard_map/all_to_all | solution.py:43
  344.8 0.0 all-reduce.5.cloned.1.call-start
  344.9 2.5 convolution_convert_fusion
  347.4 0.0 all-reduce.5.cloned.1.call-update
  347.4 1.6 fusion.9
  349.0 265.5 %all-reduce.5.cloned.1.call-done = bf16[1344,512]{1,0:T(8,128)(2,1)} async-done(((bf16[1344,512]{1,0:T(8,128)(2,1)}), bf16[1344,512]{1,0:T(8,128)(2,1)}) %all-reduce.5.cloned.1.call-update) | async-done | bytes 1376272 | tf_op jit(solution)/shard_map/psum | solution.py:36
  614.5 0.0 all-to-all-done.1
  614.5 1.3 fusion
  615.8 1.3 copy.15
Async XLA Ops:
  7.2 1.6 copy-start
  7.2 304.0 %all-reduce.3.cloned.1.call-start = ((), (), s32[]{:S(2)}) async-start(), calls=%async_computation.2 | async-start | bytes 5505024 | tf_op jit(solution)/shard_map/psum | solution.py:15
  13.3 297.9 %copy-start.2 = (f32[1,42,1024]{2,0,1:T(1,128)S(1)}, f32[1,42,1024]{2,0,1:T(1,128)}, u32[]{:S(2)}) copy-start(f32[1,42,1024]{2,0,1:T(1,128)} %param.10) | copy-start | bytes 516100
  13.3 297.9 %copy-start.3 = (bf16[1,42,1024]{2,1,0:T(8,128)(2,1)S(1)}, bf16[1,42,1024]{2,1,0:T(8,128)(2,1)}, u32[]{:S(2)}) copy-start(bf16[1,42,1024]{2,1,0:T(8,128)(2,1)} %param.9) | copy-start | bytes 258052
  331.5 1.2 copy-start.1
  332.8 281.7 %all-to-all-start.1 = ((bf16[16,1344,32]{1,2,0:T(8,128)(2,1)}), bf16[16,1344,32]{1,2,0:T(8,128)(2,1)S(1)}, u32[]{:S(2)}, u32[]{:S(2)}) async-start(bf16[16,1344,32]{1,2,0:T(8,128)(2,1)} %stack.3), calls=%async_computation.1 | async-start | bytes 2883584 | tf_op jit(solution)/shard_map/all_to_all | solution.py:43
  344.8 269.7 %all-reduce.5.cloned.1.call-start = ((), (), s32[]{:S(2)}) async-start(), calls=%async_computation.3 | async-start | bytes 2752512 | tf_op jit(solution)/shard_map/psum | solution.py:36
Sparse Core Ops, SparseCore 0:
  13.4 297.6 all-reduce.2
  348.6 265.8 all-reduce.4
